TPU v7x, 256 devices: a whole 4x4x8 slice. The times are simulated.
256 devices in a mesh: layer: 2 (over core), row: 8 (over z_hi, y), col: 16 (over x, z_lo).
Axes of the slice: x: 4, y: 4, z: 8 (z_hi: 2, z_lo: 4; z = z_hi * 4 + z_lo), core: 2. Of those that a mesh axis runs over, the one named last changes fastest.
Arguments:
- amplitudes: bfloat16 [512, 128, 128], P(('row', 'col')), may hold values from -6 to 6
- integrals: bfloat16 [32768, 128, 128], P(('layer', 'row', 'col')), may hold values from -0.1875 to 0.1875
- amp_index: int32 [4096, 48], P(('layer', 'row', 'col')), may hold values from 0 to 31
- left_index: int32 [4096, 48], P(('layer', 'row', 'col')), may hold values from 0 to 127, as said below
- right_index: int32 [4096, 48], P(('layer', 'row', 'col')), may hold values from 0 to 127, as said below
- dest_col: int32 [2048, 1], P(('row', 'col')), may hold values from 0 to 15; in each aligned block of 16 rows (0 to 15, 16 to 31, ...) at most 2 rows name the same one
- owner_slot: int32 [2048], P(('row', 'col')), may hold values from 0 to 7
Outputs:
- ladder: float32 [1024, 128, 128], P(('row', 'col'))
Inputs may be any that keep to these rules, and one draw needn't show every extreme that they name: `dest_col`: among the 16 result tiles of one index of row and col, no owner column appears more than 2 times, and some column appears exactly 2 times. A term's amplitude tile is number amp_index among the tiles of the devices with the same col index, counted row by row. A term's left and right integral tiles belong to one auxiliary function: left_index // 2 == right_index // 2. right_index // 2 == left_index // 2 for every term.
All inputs are finite; a program needn't handle non-finite values.
Results may differ from a plain program's by a relative error of at most 0.0029.
Values may be sent and summed in bfloat16 or wider, within the bound.
A program may use at most 64 MiB of HBM per device.

v0:
```python
import jax
import jax.numpy as jnp
from jax import lax
from jax.sharding import PartitionSpec as P

OWN = 8
CAP = 2


def select_tiles(stack_flat, picks, count, tile_edge):
    onehot = (picks[:, None] == jnp.arange(count, dtype=jnp.int32)[None, :]).astype(jnp.bfloat16)
    chosen = jnp.dot(onehot, stack_flat, preferred_element_type=jnp.float32).astype(jnp.bfloat16)
    return chosen.reshape(picks.shape[0], tile_edge, tile_edge)


def shards(amplitudes, integrals, amp_index, left_index, right_index, dest_col, owner_slot):
    columns = lax.axis_size("col")
    slot_count = dest_col.shape[0]
    tile_edge = integrals.shape[1]
    gathered = lax.all_gather(amplitudes, "row", axis=0, tiled=True)
    amp_total = gathered.shape[0]
    int_total = integrals.shape[0]
    amp_flat = gathered.reshape(amp_total, tile_edge * tile_edge)
    int_flat = integrals.reshape(int_total, tile_edge * tile_edge)

    def one_slot(operand_list):
        amp_ids, left_ids, right_ids = operand_list
        amp_tiles = select_tiles(amp_flat, amp_ids, amp_total, tile_edge)
        right_tiles = select_tiles(int_flat, right_ids, int_total, tile_edge)
        middle_product = jnp.einsum(
            "tcd,ted->tce", amp_tiles, right_tiles, preferred_element_type=jnp.float32
        ).astype(jnp.bfloat16)
        left_tile_blocks = select_tiles(int_flat, left_ids, int_total, tile_edge)
        return jnp.einsum(
            "dov,dvh->oh", left_tile_blocks, middle_product, preferred_element_type=jnp.float32
        )

    partials = lax.map(one_slot, (amp_index, left_index, right_index))
    target = dest_col[:, 0]
    counter = jnp.arange(slot_count, dtype=jnp.int32)
    earlier = (target[:, None] == target[None, :]) & (counter[None, :] < counter[:, None])
    position_in = jnp.sum(earlier.astype(jnp.int32), axis=1)
    position = target * CAP + position_in
    placing = (position[None, :] == jnp.arange(columns * CAP, dtype=jnp.int32)[:, None]).astype(
        jnp.float32
    )
    buffer = jnp.dot(
        placing,
        partials.reshape(slot_count, tile_edge * tile_edge),
        precision=lax.Precision.HIGHEST,
        preferred_element_type=jnp.float32,
    )
    buffer = buffer.reshape(columns, CAP, tile_edge, tile_edge)
    labels = (
        jnp.full((columns * CAP,), OWN, jnp.int32)
        .at[position]
        .set(owner_slot)
        .reshape(columns, CAP)
    )
    tiles_in, labels_in = (
        lax.all_to_all(buffer, "col", split_axis=0, concat_axis=0, tiled=True),
        lax.all_to_all(labels, "col", split_axis=0, concat_axis=0, tiled=True),
    )
    flattened = tiles_in.reshape(-1, tile_edge * tile_edge)
    owner_mask = (
        labels_in.reshape(-1)[:, None] == jnp.arange(OWN, dtype=jnp.int32)[None, :]
    ).astype(jnp.float32)
    owned_tiles = jnp.dot(
        owner_mask.T, flattened, precision=lax.Precision.HIGHEST, preferred_element_type=jnp.float32
    )
    owned_tiles = lax.psum(owned_tiles, "layer")
    return owned_tiles.reshape(OWN, tile_edge, tile_edge)


def solution(mesh):
    placed = (
        P(("row", "col"), None, None),
        P(("layer", "row", "col"), None, None),
        P(("layer", "row", "col"), None),
        P(("layer", "row", "col"), None),
        P(("layer", "row", "col"), None),
        P(("row", "col"), None),
        P(("row", "col")),
    )
    return jax.shard_map(
        shards, mesh=mesh, in_specs=placed, out_specs=P(("row", "col"), None, None), check_vma=False
    )
```

profile of v0, /device:TPU:1, one launch (start us, length us, event | category | flops | bytes accessed | tf_op | source)
XLA Modules:
  0.0 384.1 jit_solution(10383428219554340299)
XLA Ops:
  10.3 9.0 %all-to-all-start = ((s32[16,1,2]{2,1,0:T(1,128)}), s32[16,1,2]{2,1,0:T(1,128)S(1)}, u32[]{:S(2)}, u32[]{:S(2)}) async-start(s32[16,1,2]{2,1,0:T(1,128)} %bitcast.8), calls=%async_computation | async-start | bytes 16384 | tf_op jit(solution)/shard_map/all_to_all | solution.py:62
  19.3 7.7 %copy.44 = bf16[16,8,128,128]{3,1,2,0:T(8,128)(2,1)} copy(bf16[16,8,128,128]{3,2,1,0:T(8,128)(2,1)} %bitcast.108) | data formatting | bytes 8388608
  27.0 47.3 %all-gather.2.cloned.1.call-done = bf16[32,128,128]{2,1,0:T(8,128)(2,1)} async-done(((bf16[4,128,128]{2,1,0:T(8,128)(2,1)}), bf16[32,128,128]{2,1,0:T(8,128)(2,1)}) %all-gather.2.cloned.1.call-update) | async-done | bytes 1048592 | tf_op jit(solution)/shard_map/all_gather | solution.py:20
  77.2 210.3 %while.10 = (s32[]{:T(128)}, f32[16,128,128]{2,1,0:T(8,128)}, s32[16,48]{1,0:T(8,128)}, bf16[128,16384]{1,0:T(8,128)(2,1)}, s32[16,48]{1,0:T(8,128)}, /*index=5*...) while((s32[]{:T(128)}, f32[16,128,128]{2,1,0:T(8,128)}, s32[16,48]{1,0:T(8,128)}, ...), condition=%wide.region_3.4_spmd, body=%wide.region_2.3_spmd.sunk | while | flops 858797568 | bytes 45156664 | solution.py:38
  86.7 3.7 fusion.58
  91.1 2.9 fusion.54
  99.8 3.7 fusion.58
  113.0 3.7 fusion.58
  117.3 2.9 fusion.54
  126.1 3.7 fusion.58
  130.5 2.9 fusion.54
  139.3 3.7 fusion.58
  152.4 3.7 fusion.58
  156.8 2.9 fusion.54
  165.6 3.7 fusion.58
  169.9 2.9 fusion.54
  178.7 3.7 fusion.58
  183.1 2.9 fusion.54
  191.9 3.7 fusion.58
  205.0 3.7 fusion.58
  209.4 2.9 fusion.54
  218.1 3.7 fusion.58
  222.5 2.9 fusion.54
  231.3 3.7 fusion.58
  235.7 2.9 fusion.54
  244.4 3.7 fusion.58
  257.6 3.7 fusion.58
  270.7 3.7 fusion.58
  283.9 3.7 fusion.58
  292.2 4.5 %all-to-all-start.1 = ((f32[16,2,128,128]{3,2,1,0:T(8,128)}), f32[16,2,128,128]{3,2,1,0:T(8,128)S(1)}, u32[]{:S(2)}, u32[]{:S(2)}) async-start(f32[16,2,128,128]{3,2,1,0:T(8,128)} %copy.18), calls=%async_computation.1 | async-start | bytes 4194304 | tf_op jit(solution)/shard_map/all_to_all | solution.py:61
  298.2 48.2 %all-to-all-done.1 = f32[16,2,128,128]{3,2,1,0:T(8,128)S(1)} async-done(((f32[16,2,128,128]{3,2,1,0:T(8,128)}), f32[16,2,128,128]{3,2,1,0:T(8,128)S(1)}, u32[]{:S(2)}, u32[]{:S(2)}) %all-to-all-start.1) | async-done | bytes 2097184 | tf_op jit(solution)/shard_map/all_to_all | solution.py:61
  349.4 26.0 %all-reduce.2.cloned.1.call-done = f32[8,128,128]{2,1,0:T(8,128)} async-done(((f32[8,128,128]{2,1,0:T(8,128)}), f32[8,128,128]{2,1,0:T(8,128)}) %all-reduce.2.cloned.1.call-update) | async-done | bytes 524304 | tf_op jit(solution)/shard_map/psum | solution.py:71
  (174 shorter events, 142.3 us)
Async XLA Ops:
  6.5 67.8 %all-gather.2.cloned.1.call-start = ((), (), s32[]{:S(2)}) async-start(), calls=%async_computation.2 | async-start | bytes 1179648 | tf_op jit(solution)/shard_map/all_gather | solution.py:20
  10.3 281.9 %all-to-all-start = ((s32[16,1,2]{2,1,0:T(1,128)}), s32[16,1,2]{2,1,0:T(1,128)S(1)}, u32[]{:S(2)}, u32[]{:S(2)}) async-start(s32[16,1,2]{2,1,0:T(1,128)} %bitcast.8), calls=%async_computation | async-start | bytes 16384 | tf_op jit(solution)/shard_map/all_to_all | solution.py:62
  19.3 7.7 %copy-start.1 = (s32[16,1]{0,1:T(1,128)S(1)}, s32[16,1]{0,1:T(1,128)}, u32[]{:S(2)}) copy-start(s32[16,1]{0,1:T(1,128)} %param.14) | copy-start | bytes 196
  81.2 3.1 copy-start
  94.4 3.1 copy-start
  107.5 3.1 copy-start
  120.7 3.1 copy-start
  133.8 3.1 copy-start
  147.0 3.1 copy-start
  160.1 3.1 copy-start
  173.3 3.1 copy-start
  186.4 3.1 copy-start
  199.6 3.1 copy-start
  212.7 3.1 copy-start
  225.8 3.1 copy-start
  239.0 3.1 copy-start
  252.1 3.1 copy-start
  265.3 3.1 copy-start
  278.4 3.1 copy-start
  292.2 54.3 %all-to-all-start.1 = ((f32[16,2,128,128]{3,2,1,0:T(8,128)}), f32[16,2,128,128]{3,2,1,0:T(8,128)S(1)}, u32[]{:S(2)}, u32[]{:S(2)}) async-start(f32[16,2,128,128]{3,2,1,0:T(8,128)} %copy.18), calls=%async_computation.1 | async-start | bytes 4194304 | tf_op jit(solution)/shard_map/all_to_all | solution.py:61
  296.7 78.7 %all-reduce.2.cloned.1.call-start = ((), (), s32[]{:S(2)}) async-start(), calls=%async_computation.3 | async-start | bytes 1048576 | tf_op jit(solution)/shard_map/psum | solution.py:71
Sparse Core Ops, SparseCore 0:
  10.0 64.2 all-gather.1
  349.6 25.8 all-reduce.1
where the time goes:
time: 386 us; the launch traced here: 384 us
  matrix products  153 us (40%)
  waiting for transfers between devices  122 us (32%)
  local copies, waits for them, and re-layouts  78.2 us (20%)
  starting transfers between devices  13.8 us (4%)
  between operations  13.5 us (3%)
    dot_general x48, matrix products, select_tiles(): jnp.dot(onehot, stack_flat, preferred_element_type=jnp.float32)  90.2 us
    dot_general x16, matrix products, one_slot(): jnp.einsum('dov,dvh->oh', left_tile_blocks, middle_product, preferred_ele...  58.6 us
    all_to_all x1, waiting for transfers between devices, shards(): lax.all_to_all(buffer, 'col', split_axis=0, concat_axis=0, tiled=True)  48.2 us
    all_gather x1, waiting for transfers between devices, shards(): gathered = lax.all_gather(amplitudes, 'row', axis=0, tiled=True)  47.3 us
    while x80, local copies, waits for them, and re-layouts  38.3 us
    psum x1, waiting for transfers between devices, shards(): owned_tiles = lax.psum(owned_tiles, 'layer')  26 us
    eq x32, local copies, waits for them, and re-layouts, select_tiles(): picks[:, None] == jnp.arange(count, dtype=jnp.int32)[None, :]  22.5 us
    unnamed x5, local copies, waits for them, and re-layouts  12.5 us
  transfers between devices with their start and end apart: 4, of which 3 were waited for; matrix products, arithmetic and copies ran while one was open for 59% of the time, Pallas kernels for 0%

commit v1 on v0

--- a/solution.py
+++ b/solution.py
@@ -17,7 +17,12 @@
     columns = lax.axis_size("col")
     slot_count = dest_col.shape[0]
     tile_edge = integrals.shape[1]
-    gathered = lax.all_gather(amplitudes, "row", axis=0, tiled=True)
+    gathered = jnp.concatenate(
+        lax.all_to_all(
+            jnp.stack([amplitudes for _ in range(lax.axis_size("row"))], axis=0), "row", 0, 0
+        ),
+        axis=0,
+    )
     amp_total = gathered.shape[0]
     int_total = integrals.shape[0]
     amp_flat = gathered.reshape(amp_total, tile_edge * tile_edge)

time: 386 us -> 368 us (0.953)
  waiting for transfers between devices: 122 us -> 84.5 us
  starting transfers between devices: 13.8 us -> 33.2 us
    all_gather x1 -> x0, waiting for transfers between devices: 47.3 us -> none  [shards(): gathered = lax.all_gather(amplitudes, 'row', axis=0, tiled=True)]
    all_to_all x0 -> x1, starting transfers between devices: none -> 11.6 us  [shards(): lax.all_to_all(jnp.stack([amplitudes for _ in range(lax.axis_size('row'))...]
    all_to_all x0 -> x1, waiting for transfers between devices: none -> 9.43 us  [shards(): lax.all_to_all(jnp.stack([amplitudes for _ in range(lax.axis_size('row'))...]
    all_to_all x1, starting transfers between devices: 9.01 us -> 14.4 us  [shards(): lax.all_to_all(labels, 'col', split_axis=0, concat_axis=0, tiled=True)]
  transfers between devices with their start and end apart: 4 -> 4, of which waited for: 3 -> 3; matrix products, arithmetic and copies ran while one was open for 59% -> 62% of each run, Pallas kernels for 0% -> 0%
where the time goes in v1:
time: 368 us; the launch traced here: 365 us
  matrix products  154 us (42%)
  waiting for transfers between devices  84.5 us (23%)
  local copies, waits for them, and re-layouts  79.2 us (22%)
  starting transfers between devices  33.2 us (9%)
  between operations  13.5 us (4%)
    dot_general x48, matrix products, select_tiles(): jnp.dot(onehot, stack_flat, preferred_element_type=jnp.float32)  90.2 us
    dot_general x16, matrix products, one_slot(): jnp.einsum('dov,dvh->oh', left_tile_blocks, middle_product, preferred_ele...  58.6 us
    all_to_all x1, waiting for transfers between devices, shards(): lax.all_to_all(buffer, 'col', split_axis=0, concat_axis=0, tiled=True)  48.2 us
    while x80, local copies, waits for them, and re-layouts  38.4 us
    psum x1, waiting for transfers between devices, shards(): owned_tiles = lax.psum(owned_tiles, 'layer')  26.8 us
    eq x32, local copies, waits for them, and re-layouts, select_tiles(): picks[:, None] == jnp.arange(count, dtype=jnp.int32)[None, :]  22.5 us
    all_to_all x1, starting transfers between devices, shards(): lax.all_to_all(labels, 'col', split_axis=0, concat_axis=0, tiled=True)  14.4 us
    all_to_all x1, starting transfers between devices, shards(): lax.all_to_all(jnp.stack([amplitudes for _ in range(lax.axis_size('row'))...  11.6 us
  transfers between devices with their start and end apart: 4, of which 3 were waited for; matrix products, arithmetic and copies ran while one was open for 62% of the time, Pallas kernels for 0%

profile of v1, /device:TPU:1, one launch (start us, length us, event | category | flops | bytes accessed | tf_op | source)
XLA Modules:
  0.0 365.5 jit_solution(6332856486099347441)
XLA Ops:
  8.7 11.6 %all-to-all-start.1 = ((bf16[8,4,128,128]{3,2,1,0:T(8,128)(2,1)}), bf16[8,4,128,128]{3,2,1,0:T(8,128)(2,1)S(1)}, u32[]{:S(2)}, u32[]{:S(2)}) async-start(bf16[8,4,128,128]{3,2,1,0:T(8,128)(2,1)} %stack.2), calls=%async_computation.1 | async-start | bytes 2097152 | tf_op jit(solution)/shard_map/all_to_all | solution.py:21
  20.3 7.7 %copy.44 = bf16[16,8,128,128]{3,1,2,0:T(8,128)(2,1)} copy(bf16[16,8,128,128]{3,2,1,0:T(8,128)(2,1)} %bitcast.109) | data formatting | bytes 8388608
  29.6 9.4 %all-to-all-done.1 = bf16[8,4,128,128]{3,2,1,0:T(8,128)(2,1)S(1)} async-done(((bf16[8,4,128,128]{3,2,1,0:T(8,128)(2,1)}), bf16[8,4,128,128]{3,2,1,0:T(8,128)(2,1)S(1)}, u32[]{:S(2)}, u32[]{:S(2)}) %all-to-all-start.1) | async-done | bytes 1048608 | tf_op jit(solution)/shard_map/all_to_all | solution.py:21
  39.1 14.4 %all-to-all-start = ((s32[16,1,2]{2,1,0:T(1,128)}), s32[16,1,2]{2,1,0:T(1,128)S(1)}, u32[]{:S(2)}, u32[]{:S(2)}) async-start(s32[16,1,2]{2,1,0:T(1,128)} %bitcast.8), calls=%async_computation | async-start | bytes 16384 | tf_op jit(solution)/shard_map/all_to_all | solution.py:67
  55.1 210.5 %while.10 = (s32[]{:T(128)}, f32[16,128,128]{2,1,0:T(8,128)}, s32[16,48]{1,0:T(8,128)}, bf16[128,16384]{1,0:T(8,128)(2,1)}, s32[16,48]{1,0:T(8,128)}, /*index=5*...) while((s32[]{:T(128)}, f32[16,128,128]{2,1,0:T(8,128)}, s32[16,48]{1,0:T(8,128)}, ...), condition=%wide.region_3.4_spmd, body=%wide.region_2.3_spmd.sunk | while | flops 858797568 | bytes 45156664 | solution.py:43
  64.6 3.7 %fusion.58 = f32[16,128,128]{2,1,0:T(8,128)} fusion(f32[16,128,128]{2,1,0:T(8,128)} %get-tuple-element.115, s32[]{:T(128)} %get-tuple-element.114, bf16[48,128,128]{2,1,0:T(8,128)(2,1)S(1)} %bitcast.105, bf16[48,128,128]{2,1,0:T(8,128)(2,1)S(1)} %bitcast.106, bf16[48,128,128]{2,1,0:T(8,128)(2,1)} %bitcast.107), kind=kOutput, calls=%fused_computation.10.clone.1 | convolution fusion | flops 403439616 | bytes 4784640 | tf_op jit(solution)/shard_map/while/body/eval_jaxpr/dov,dvh->oh/dot_general | solution.py:39
  69.0 2.9 fusion.54
  77.8 3.7 %fusion.58 = f32[16,128,128]{2,1,0:T(8,128)} fusion(f32[16,128,128]{2,1,0:T(8,128)} %get-tuple-element.115, s32[]{:T(128)} %get-tuple-element.114, bf16[48,128,128]{2,1,0:T(8,128)(2,1)S(1)} %bitcast.105, bf16[48,128,128]{2,1,0:T(8,128)(2,1)S(1)} %bitcast.106, bf16[48,128,128]{2,1,0:T(8,128)(2,1)} %bitcast.107), kind=kOutput, calls=%fused_computation.10.clone.1 | convolution fusion | flops 403439616 | bytes 4784640 | tf_op jit(solution)/shard_map/while/body/eval_jaxpr/dov,dvh->oh/dot_general | solution.py:39
  82.2 2.9 fusion.54
  90.9 3.7 %fusion.58 = f32[16,128,128]{2,1,0:T(8,128)} fusion(f32[16,128,128]{2,1,0:T(8,128)} %get-tuple-element.115, s32[]{:T(128)} %get-tuple-element.114, bf16[48,128,128]{2,1,0:T(8,128)(2,1)S(1)} %bitcast.105, bf16[48,128,128]{2,1,0:T(8,128)(2,1)S(1)} %bitcast.106, bf16[48,128,128]{2,1,0:T(8,128)(2,1)} %bitcast.107), kind=kOutput, calls=%fused_computation.10.clone.1 | convolution fusion | flops 403439616 | bytes 4784640 | tf_op jit(solution)/shard_map/while/body/eval_jaxpr/dov,dvh->oh/dot_general | solution.py:39
  95.3 2.9 fusion.54
  104.1 3.7 %fusion.58 = f32[16,128,128]{2,1,0:T(8,128)} fusion(f32[16,128,128]{2,1,0:T(8,128)} %get-tuple-element.115, s32[]{:T(128)} %get-tuple-element.114, bf16[48,128,128]{2,1,0:T(8,128)(2,1)S(1)} %bitcast.105, bf16[48,128,128]{2,1,0:T(8,128)(2,1)S(1)} %bitcast.106, bf16[48,128,128]{2,1,0:T(8,128)(2,1)} %bitcast.107), kind=kOutput, calls=%fused_computation.10.clone.1 | convolution fusion | flops 403439616 | bytes 4784640 | tf_op jit(solution)/shard_map/while/body/eval_jaxpr/dov,dvh->oh/dot_general | solution.py:39
  117.2 3.7 %fusion.58 = f32[16,128,128]{2,1,0:T(8,128)} fusion(f32[16,128,128]{2,1,0:T(8,128)} %get-tuple-element.115, s32[]{:T(128)} %get-tuple-element.114, bf16[48,128,128]{2,1,0:T(8,128)(2,1)S(1)} %bitcast.105, bf16[48,128,128]{2,1,0:T(8,128)(2,1)S(1)} %bitcast.106, bf16[48,128,128]{2,1,0:T(8,128)(2,1)} %bitcast.107), kind=kOutput, calls=%fused_computation.10.clone.1 | convolution fusion | flops 403439616 | bytes 4784640 | tf_op jit(solution)/shard_map/while/body/eval_jaxpr/dov,dvh->oh/dot_general | solution.py:39
  121.6 2.9 fusion.54
  130.4 3.7 %fusion.58 = f32[16,128,128]{2,1,0:T(8,128)} fusion(f32[16,128,128]{2,1,0:T(8,128)} %get-tuple-element.115, s32[]{:T(128)} %get-tuple-element.114, bf16[48,128,128]{2,1,0:T(8,128)(2,1)S(1)} %bitcast.105, bf16[48,128,128]{2,1,0:T(8,128)(2,1)S(1)} %bitcast.106, bf16[48,128,128]{2,1,0:T(8,128)(2,1)} %bitcast.107), kind=kOutput, calls=%fused_computation.10.clone.1 | convolution fusion | flops 403439616 | bytes 4784640 | tf_op jit(solution)/shard_map/while/body/eval_jaxpr/dov,dvh->oh/dot_general | solution.py:39
  134.8 2.9 fusion.54
  143.5 3.7 %fusion.58 = f32[16,128,128]{2,1,0:T(8,128)} fusion(f32[16,128,128]{2,1,0:T(8,128)} %get-tuple-element.115, s32[]{:T(128)} %get-tuple-element.114, bf16[48,128,128]{2,1,0:T(8,128)(2,1)S(1)} %bitcast.105, bf16[48,128,128]{2,1,0:T(8,128)(2,1)S(1)} %bitcast.106, bf16[48,128,128]{2,1,0:T(8,128)(2,1)} %bitcast.107), kind=kOutput, calls=%fused_computation.10.clone.1 | convolution fusion | flops 403439616 | bytes 4784640 | tf_op jit(solution)/shard_map/while/body/eval_jaxpr/dov,dvh->oh/dot_general | solution.py:39
  156.7 3.7 %fusion.58 = f32[16,128,128]{2,1,0:T(8,128)} fusion(f32[16,128,128]{2,1,0:T(8,128)} %get-tuple-element.115, s32[]{:T(128)} %get-tuple-element.114, bf16[48,128,128]{2,1,0:T(8,128)(2,1)S(1)} %bitcast.105, bf16[48,128,128]{2,1,0:T(8,128)(2,1)S(1)} %bitcast.106, bf16[48,128,128]{2,1,0:T(8,128)(2,1)} %bitcast.107), kind=kOutput, calls=%fused_computation.10.clone.1 | convolution fusion | flops 403439616 | bytes 4784640 | tf_op jit(solution)/shard_map/while/body/eval_jaxpr/dov,dvh->oh/dot_general | solution.py:39
  169.9 3.7 %fusion.58 = f32[16,128,128]{2,1,0:T(8,128)} fusion(f32[16,128,128]{2,1,0:T(8,128)} %get-tuple-element.115, s32[]{:T(128)} %get-tuple-element.114, bf16[48,128,128]{2,1,0:T(8,128)(2,1)S(1)} %bitcast.105, bf16[48,128,128]{2,1,0:T(8,128)(2,1)S(1)} %bitcast.106, bf16[48,128,128]{2,1,0:T(8,128)(2,1)} %bitcast.107), kind=kOutput, calls=%fused_computation.10.clone.1 | convolution fusion | flops 403439616 | bytes 4784640 | tf_op jit(solution)/shard_map/while/body/eval_jaxpr/dov,dvh->oh/dot_general | solution.py:39
  183.0 3.7 %fusion.58 = f32[16,128,128]{2,1,0:T(8,128)} fusion(f32[16,128,128]{2,1,0:T(8,128)} %get-tuple-element.115, s32[]{:T(128)} %get-tuple-element.114, bf16[48,128,128]{2,1,0:T(8,128)(2,1)S(1)} %bitcast.105, bf16[48,128,128]{2,1,0:T(8,128)(2,1)S(1)} %bitcast.106, bf16[48,128,128]{2,1,0:T(8,128)(2,1)} %bitcast.107), kind=kOutput, calls=%fused_computation.10.clone.1 | convolution fusion | flops 403439616 | bytes 4784640 | tf_op jit(solution)/shard_map/while/body/eval_jaxpr/dov,dvh->oh/dot_general | solution.py:39
  196.2 3.7 %fusion.58 = f32[16,128,128]{2,1,0:T(8,128)} fusion(f32[16,128,128]{2,1,0:T(8,128)} %get-tuple-element.115, s32[]{:T(128)} %get-tuple-element.114, bf16[48,128,128]{2,1,0:T(8,128)(2,1)S(1)} %bitcast.105, bf16[48,128,128]{2,1,0:T(8,128)(2,1)S(1)} %bitcast.106, bf16[48,128,128]{2,1,0:T(8,128)(2,1)} %bitcast.107), kind=kOutput, calls=%fused_computation.10.clone.1 | convolution fusion | flops 403439616 | bytes 4784640 | tf_op jit(solution)/shard_map/while/body/eval_jaxpr/dov,dvh->oh/dot_general | solution.py:39
  200.5 2.9 fusion.54
  209.3 3.7 %fusion.58 = f32[16,128,128]{2,1,0:T(8,128)} fusion(f32[16,128,128]{2,1,0:T(8,128)} %get-tuple-element.115, s32[]{:T(128)} %get-tuple-element.114, bf16[48,128,128]{2,1,0:T(8,128)(2,1)S(1)} %bitcast.105, bf16[48,128,128]{2,1,0:T(8,128)(2,1)S(1)} %bitcast.106, bf16[48,128,128]{2,1,0:T(8,128)(2,1)} %bitcast.107), kind=kOutput, calls=%fused_computation.10.clone.1 | convolution fusion | flops 403439616 | bytes 4784640 | tf_op jit(solution)/shard_map/while/body/eval_jaxpr/dov,dvh->oh/dot_general | solution.py:39
  222.5 3.7 %fusion.58 = f32[16,128,128]{2,1,0:T(8,128)} fusion(f32[16,128,128]{2,1,0:T(8,128)} %get-tuple-element.115, s32[]{:T(128)} %get-tuple-element.114, bf16[48,128,128]{2,1,0:T(8,128)(2,1)S(1)} %bitcast.105, bf16[48,128,128]{2,1,0:T(8,128)(2,1)S(1)} %bitcast.106, bf16[48,128,128]{2,1,0:T(8,128)(2,1)} %bitcast.107), kind=kOutput, calls=%fused_computation.10.clone.1 | convolution fusion | flops 403439616 | bytes 4784640 | tf_op jit(solution)/shard_map/while/body/eval_jaxpr/dov,dvh->oh/dot_general | solution.py:39
  226.8 2.9 fusion.54
  235.6 3.7 %fusion.58 = f32[16,128,128]{2,1,0:T(8,128)} fusion(f32[16,128,128]{2,1,0:T(8,128)} %get-tuple-element.115, s32[]{:T(128)} %get-tuple-element.114, bf16[48,128,128]{2,1,0:T(8,128)(2,1)S(1)} %bitcast.105, bf16[48,128,128]{2,1,0:T(8,128)(2,1)S(1)} %bitcast.106, bf16[48,128,128]{2,1,0:T(8,128)(2,1)} %bitcast.107), kind=kOutput, calls=%fused_computation.10.clone.1 | convolution fusion | flops 403439616 | bytes 4784640 | tf_op jit(solution)/shard_map/while/body/eval_jaxpr/dov,dvh->oh/dot_general | solution.py:39
  248.8 3.7 %fusion.58 = f32[16,128,128]{2,1,0:T(8,128)} fusion(f32[16,128,128]{2,1,0:T(8,128)} %get-tuple-element.115, s32[]{:T(128)} %get-tuple-element.114, bf16[48,128,128]{2,1,0:T(8,128)(2,1)S(1)} %bitcast.105, bf16[48,128,128]{2,1,0:T(8,128)(2,1)S(1)} %bitcast.106, bf16[48,128,128]{2,1,0:T(8,128)(2,1)} %bitcast.107), kind=kOutput, calls=%fused_computation.10.clone.1 | convolution fusion | flops 403439616 | bytes 4784640 | tf_op jit(solution)/shard_map/while/body/eval_jaxpr/dov,dvh->oh/dot_general | solution.py:39
  253.1 2.9 fusion.54
  261.9 3.7 %fusion.58 = f32[16,128,128]{2,1,0:T(8,128)} fusion(f32[16,128,128]{2,1,0:T(8,128)} %get-tuple-element.115, s32[]{:T(128)} %get-tuple-element.114, bf16[48,128,128]{2,1,0:T(8,128)(2,1)S(1)} %bitcast.105, bf16[48,128,128]{2,1,0:T(8,128)(2,1)S(1)} %bitcast.106, bf16[48,128,128]{2,1,0:T(8,128)(2,1)} %bitcast.107), kind=kOutput, calls=%fused_computation.10.clone.1 | convolution fusion | flops 403439616 | bytes 4784640 | tf_op jit(solution)/shard_map/while/body/eval_jaxpr/dov,dvh->oh/dot_general | solution.py:39
  270.3 7.0 %all-to-all-start.2 = ((f32[16,2,128,128]{3,2,1,0:T(8,128)}), f32[16,2,128,128]{3,2,1,0:T(8,128)S(1)}, u32[]{:S(2)}, u32[]{:S(2)}) async-start(f32[16,2,128,128]{3,2,1,0:T(8,128)} %copy.18), calls=%async_computation.2 | async-start | bytes 4194304 | tf_op jit(solution)/shard_map/all_to_all | solution.py:66
  278.7 48.2 %all-to-all-done.2 = f32[16,2,128,128]{3,2,1,0:T(8,128)S(1)} async-done(((f32[16,2,128,128]{3,2,1,0:T(8,128)}), f32[16,2,128,128]{3,2,1,0:T(8,128)S(1)}, u32[]{:S(2)}, u32[]{:S(2)}) %all-to-all-start.2) | async-done | bytes 2097184 | tf_op jit(solution)/shard_map/all_to_all | solution.py:66
  329.9 26.8 %all-reduce.2.cloned.1.call-done = f32[8,128,128]{2,1,0:T(8,128)} async-done(((f32[8,128,128]{2,1,0:T(8,128)}), f32[8,128,128]{2,1,0:T(8,128)}) %all-reduce.2.cloned.1.call-update) | async-done | bytes 524304 | tf_op jit(solution)/shard_map/psum | solution.py:76
  (174 shorter events, 144.1 us)
Async XLA Ops:
  8.7 30.4 %all-to-all-start.1 = ((bf16[8,4,128,128]{3,2,1,0:T(8,128)(2,1)}), bf16[8,4,128,128]{3,2,1,0:T(8,128)(2,1)S(1)}, u32[]{:S(2)}, u32[]{:S(2)}) async-start(bf16[8,4,128,128]{3,2,1,0:T(8,128)(2,1)} %stack.2), calls=%async_computation.1 | async-start | bytes 2097152 | tf_op jit(solution)/shard_map/all_to_all | solution.py:21
  20.3 7.7 %copy-start.1 = (s32[16,1]{0,1:T(1,128)S(1)}, s32[16,1]{0,1:T(1,128)}, u32[]{:S(2)}) copy-start(s32[16,1]{0,1:T(1,128)} %param.14) | copy-start | bytes 196
  39.1 231.2 %all-to-all-start = ((s32[16,1,2]{2,1,0:T(1,128)}), s32[16,1,2]{2,1,0:T(1,128)S(1)}, u32[]{:S(2)}, u32[]{:S(2)}) async-start(s32[16,1,2]{2,1,0:T(1,128)} %bitcast.8), calls=%async_computation | async-start | bytes 16384 | tf_op jit(solution)/shard_map/all_to_all | solution.py:67
  59.2 3.1 copy-start
  72.3 3.1 copy-start
  85.5 3.1 copy-start
  98.6 3.1 copy-start
  111.8 3.1 copy-start
  124.9 3.1 copy-start
  138.1 3.1 copy-start
  151.2 3.1 copy-start
  164.4 3.1 copy-start
  177.6 3.1 copy-start
  190.7 3.1 copy-start
  203.9 3.1 copy-start
  217.0 3.1 copy-start
  230.2 3.1 copy-start
  243.3 3.1 copy-start
  256.5 3.1 copy-start
  270.3 56.7 %all-to-all-start.2 = ((f32[16,2,128,128]{3,2,1,0:T(8,128)}), f32[16,2,128,128]{3,2,1,0:T(8,128)S(1)}, u32[]{:S(2)}, u32[]{:S(2)}) async-start(f32[16,2,128,128]{3,2,1,0:T(8,128)} %copy.18), calls=%async_computation.2 | async-start | bytes 4194304 | tf_op jit(solution)/shard_map/all_to_all | solution.py:66
  277.2 79.5 %all-reduce.2.cloned.1.call-start = ((), (), s32[]{:S(2)}) async-start(), calls=%async_computation.3 | async-start | bytes 1048576 | tf_op jit(solution)/shard_map/psum | solution.py:76
Sparse Core Ops, SparseCore 0:
  330.0 26.6 all-reduce.1
